TPU v7x, 32 devices: a whole 2x2x4 slice. The times are simulated.
32 devices in a mesh: ctx: 8 (over y, x, core), chan: 4 (over z).
Axes of the slice: x: 2, y: 2, z: 4, core: 2. Of those that a mesh axis runs over, the one named last changes fastest.
Arguments:
- features: bfloat16 [3, 8192, 4096], P(None, 'chan', 'ctx'), may hold values from -6 to 6
- short_filter: float32 [3, 3, 8192], P(None, None, 'chan'), may hold values from -3.5 to 3.5
- lengths: int32 [8], P('ctx'), may hold values from 64 to 512, as said below
- offsets: int32 [8], P('ctx'), may hold values from 0 to 8128, as said below
- decay_rates: float32 [16, 1024], P(None, 'chan'), may hold values from 0 to 1, as said below
- residues: float32 [16, 1024], P(None, 'chan'), may hold values from -1 to 1
- skip_weight: float32 [8192], P('chan'), may hold values from -1 to 1
- out_weight: bfloat16 [8192, 4096], P('chan'), may hold values from -0.09375 to 0.09375
Outputs:
- projected: bfloat16 [4096, 4096], P('chan', 'ctx')
Inputs may be any that keep to these rules, and one draw needn't show every extreme that they name: `lengths`: used slots of each shard, counted from slot 0; some shard uses all 512 slots and some only 64. offsets[i] + lengths[i] <= offsets[i + 1]; the first offset is 0. `decay_rates`: positive rates.
All inputs are finite; a program needn't handle non-finite values.
Results may differ from a plain program's by a relative error of at most 0.018.
Values may be sent and summed in bfloat16 or wider, within the bound.
No kernel may reach another device: no remote copies, remote signals or barrier semaphores. Data moves between devices by JAX's collectives and lax.ppermute only.
A program may use at most 192 MiB of HBM per device.

v0:
```python
import jax
import jax.numpy as jnp
from jax import lax
from jax.sharding import PartitionSpec as P

highest = lax.Precision.HIGHEST


def passed_along(array, axis, by):
    length = lax.axis_size(axis)
    pairs = [(i, i + by) for i in range(length) if 0 <= i + by < length]
    return lax.ppermute(array, axis, pairs)


def shortened(array):
    return jax.tree.map(lambda a: a.astype(jnp.bfloat16) if a.dtype == jnp.float32 else a, array)


def block_pass(blocks, firsts, counts, decay_rows, residue):
    groups, per_group, block_count, block_width = blocks.shape
    mode_count = decay_rows.shape[0]
    rate_g = decay_rows.T
    residue_g = residue.T
    lag_index = jnp.arange(block_width)
    lag_float = lag_index.astype(jnp.float32)
    to_end = jnp.exp(-rate_g[:, None, :] * (block_width - 1.0 - lag_float)[None, :, None])
    raw_sums = lax.dot_general(
        blocks.reshape(groups, per_group * block_count, block_width),
        to_end,
        (((2,), (1,)), ((0,), (0,))),
        precision=highest,
    )
    lift = jnp.exp(rate_g[:, None, :] * (block_width - counts.astype(jnp.float32))[None, :, None])
    summary = raw_sums.reshape(groups, per_group, block_count, mode_count) * lift[:, None, :, :]
    difference = (lag_index[:, None] - lag_index[None, :]).astype(jnp.float32)
    distance = jnp.maximum(difference, 0.0)
    toeplitz = jnp.zeros((groups, block_width, block_width), jnp.float32)
    for mode_index in range(mode_count):
        toeplitz = toeplitz + residue_g[:, mode_index, None, None] * jnp.exp(
            -rate_g[:, mode_index, None, None] * distance[None]
        )
    toeplitz = jnp.where((difference >= 0.0)[None], toeplitz, 0.0)
    inner_part = lax.dot_general(blocks, toeplitz, (((3,), (2,)), ((0,), (0,))), precision=highest)
    lasts = firsts + counts.astype(jnp.float32) - 1.0
    gap_matrix = jnp.maximum(firsts[None, :] - lasts[:, None], 0.0)
    earlier_mask = lag_index[:block_count, None] < lag_index[None, :block_count]
    mixing = jnp.where(
        earlier_mask[None, None], jnp.exp(-rate_g[:, :, None, None] * gap_matrix[None, None]), 0.0
    )
    entering = jnp.einsum("gkcm,gmcb->gkbm", summary, mixing, precision=highest)
    return (inner_part, summary, entering, lasts)


def outer_pass(entering, decay_rows, residue, block_width):
    groups, per_group, block_count, mode_count = entering.shape
    rate_g = decay_rows.T
    lag_float = jnp.arange(block_width, dtype=jnp.float32)
    spread_values = residue.T[:, :, None] * jnp.exp(-rate_g[:, :, None] * lag_float[None, None, :])
    outer_part = lax.dot_general(
        entering.reshape(groups, per_group * block_count, mode_count),
        spread_values,
        (((2,), (1,)), ((0,), (0,))),
        precision=highest,
    )
    return outer_part.reshape(groups, per_group, block_count, block_width)


def shards(
    features, short_filter, lengths, offsets, decay_rates, residues, skip_weight, out_weight
):
    kernel_taps = short_filter.shape[1]
    channels = features.shape[1]
    slot_count = features.shape[2]
    groups = decay_rates.shape[1]
    per_group = channels // groups
    block_width = min(128, slot_count)
    length = lengths[0]
    tail_rows = lax.dynamic_slice_in_dim(
        features, length - (kernel_taps - 1), kernel_taps - 1, axis=2
    )
    previous = passed_along(tail_rows, "ctx", 1)
    extended = jnp.concatenate([previous, features], axis=2)
    short_conv = jnp.zeros((3, channels, slot_count), jnp.float32)
    for tap_index in range(kernel_taps):
        window_rows = lax.slice_in_dim(
            extended, kernel_taps - 1 - tap_index, kernel_taps - 1 - tap_index + slot_count, axis=2
        )
        short_conv = short_conv + short_filter[:, tap_index, :, None] * window_rows.astype(
            jnp.float32
        )
    usable = jnp.arange(slot_count) < length
    product = jnp.where(usable, short_conv[1] * short_conv[2], 0.0)
    all_lengths, all_offsets = (
        lax.all_gather(lengths, "ctx", axis=0, tiled=True),
        lax.all_gather(offsets, "ctx", axis=0, tiled=True),
    )
    ctx_count = lax.axis_size("ctx")
    rank_self = lax.axis_index("ctx")
    shared = groups // ctx_count
    decay_mine = lax.dynamic_slice_in_dim(decay_rates, rank_self * shared, shared, 1)
    residue_mine = lax.dynamic_slice_in_dim(residues, rank_self * shared, shared, 1)
    per_shard = slot_count // block_width
    within = jnp.tile(jnp.arange(per_shard) * block_width, ctx_count)
    firsts_all = jnp.repeat(all_offsets, per_shard).astype(jnp.float32) + within.astype(jnp.float32)
    counts_all = jnp.clip(jnp.repeat(all_lengths, per_shard) - within, 0, block_width)
    received = lax.all_to_all(
        product.reshape(groups, per_group, slot_count).astype(jnp.bfloat16),
        "ctx",
        split_axis=0,
        concat_axis=2,
        tiled=True,
    ).astype(jnp.float32)
    item_count = received.shape[1]
    blocks = received.reshape(shared, item_count, ctx_count * per_shard, block_width)
    inner_part, summary, entering, lasts = block_pass(
        blocks, firsts_all, counts_all, decay_mine, residue_mine
    )
    outer_part = outer_pass(entering, decay_mine, residue_mine, block_width)
    result = (inner_part + outer_part).reshape(shared, item_count, ctx_count * slot_count)
    long_conv = lax.all_to_all(
        shortened(result), "ctx", split_axis=2, concat_axis=0, tiled=True
    ).astype(result.dtype)
    long_conv = long_conv.reshape(channels, slot_count)
    mixed_rows = jnp.where(
        usable, short_conv[0] * (long_conv + skip_weight[:, None] * product), 0.0
    ).astype(jnp.bfloat16)
    return lax.psum_scatter(
        lax.dot_general(
            out_weight, mixed_rows, (((0,), (0,)), ((), ())), preferred_element_type=jnp.float32
        ).astype(jnp.bfloat16),
        "chan",
        scatter_dimension=0,
        tiled=True,
    )


def solution(mesh):
    placed = (
        P(None, "chan", "ctx"),
        P(None, None, "chan"),
        P("ctx"),
        P("ctx"),
        P(None, "chan"),
        P(None, "chan"),
        P("chan"),
        P("chan", None),
    )
    return jax.shard_map(
        shards, mesh=mesh, in_specs=placed, out_specs=P("chan", "ctx"), check_vma=False
    )
```

profile of v0, /device:TPU:0, one launch (start us, length us, event | category | flops | bytes accessed | tf_op | source)
XLA Modules:
  0.0 309.9 jit_solution(4460304330251844339)
XLA Ops:
  7.2 2.5 constant_dynamic-slice_fusion
  9.7 0.9 copy.54
  10.6 2.4 collective-permute-start
  13.6 0.6 dynamic-slice
  14.3 0.7 dynamic-update-slice.1
  15.0 0.7 dynamic-update-slice
  15.8 9.1 %all-reduce.2 = (s32[8]{0:T(128)S(1)}, s32[8]{0:T(128)S(1)}) all-reduce(s32[8]{0:T(128)S(1)} %dynamic-update-slice, s32[8]{0:T(128)S(1)} %dynamic-update-slice.1), channel_id=1, replica_groups=mesh['ctx'=8,'chan'=4] {'ctx'}, use_global_device_ids=true, to_apply=%add | all-reduce | flops 16 | bytes 128
  25.1 0.9 copy.38
  26.0 12.5 %multiply_add_fusion = f32[3,2048,512]{2,1,0:T(8,128)S(1)} fusion(bf16[3,2048,512]{2,1,0:T(8,128)(2,1)} %param.8, bf16[3,2048,2]{2,1,0:T(8,128)(2,1)S(1)} %copy.38, f32[3,2048]{1,0:T(4,128)S(1)} %get-tuple-element.46, f32[3,2048]{1,0:T(4,128)S(1)} %get-tuple-element.47, f32[3,2048]{1,0:T(4,128)S(1)} %bitcast.143), kind=kLoop, calls=%fused_computation.1 | loop fusion | flops 44040192 | bytes 18972672 | tf_op jit(solution)/shard_map/add | solution.py:88
  38.5 4.5 %copy-done.2 = f32[3,2048,512]{2,1,0:T(8,128)} copy-done((f32[3,2048,512]{2,1,0:T(8,128)}, f32[3,2048,512]{2,1,0:T(8,128)S(1)}, u32[]{:S(2)}) %copy-start.2) | copy-done | bytes 12582936
  43.1 2.5 fusion.11
  45.5 3.7 %all-to-all-start = ((bf16[256,8,512]{2,1,0:T(8,128)(2,1)}), bf16[256,8,512]{2,1,0:T(8,128)(2,1)S(1)}, u32[]{:S(2)}, u32[]{:S(2)}) async-start(bf16[256,8,512]{2,1,0:T(8,128)(2,1)} %fusion.11), calls=%async_computation | async-start | bytes 4194304 | tf_op jit(solution)/shard_map/all_to_all | solution.py:106
  50.3 25.6 %all-to-all-done = bf16[256,8,512]{2,1,0:T(8,128)(2,1)S(1)} async-done(((bf16[256,8,512]{2,1,0:T(8,128)(2,1)}), bf16[256,8,512]{2,1,0:T(8,128)(2,1)S(1)}, u32[]{:S(2)}, u32[]{:S(2)}) %all-to-all-start) | async-done | bytes 2097184 | tf_op jit(solution)/shard_map/all_to_all | solution.py:106
  75.9 1.3 copy-done.3
  77.2 3.3 %copy.39 = bf16[32,8,8,512]{3,2,1,0:T(8,128)(2,1)S(1)} copy(bf16[32,8,8,512]{3,1,0,2:T(8,128)(2,1)} %bitcast.141) | data formatting | bytes 4194304 | tf_op jit(solution)/shard_map/all_to_all | solution.py:106
  80.5 2.8 reshape_reshape.3
  83.3 2.6 reshape.334
  85.9 3.4 %fusion.128 = f32[32,256,16]{1,2,0:T(8,128)S(1)} fusion(bf16[32,256,128]{2,1,0:T(8,128)(2,1)} %reshape_reshape.3, f32[128]{0:T(128)S(1)} %convert_subtract_fusion, f32[32,16]{1,0:T(8,128)S(1)} %copy.40), kind=kOutput, calls=%fused_computation.136 | convolution fusion | flops 201392128 | bytes 2624000 | tf_op jit(solution)/shard_map/dot_general | solution.py:27
  89.7 17.6 %fusion.82 = f32[32,8,32,16]{2,1,3,0:T(8,128)} fusion(f32[32,8,32,16]{2,1,3,0:T(8,128)S(1)} %reshape.335, f32[32,32]{1,0:T(8,128)S(1)} %subtract_maximum_fusion, f32[32,16]{1,0:T(8,128)S(1)} %copy.40, pred[32,32]{1,0:T(8,128)(4,1)S(1)} %broadcast_compare_fusion, f32[32,32,16]{1,2,0:T(8,128)S(1)} %multiply_exponential_fusion), kind=kOutput, calls=%fused_computation.93 | convolution fusion | flops 51511296 | bytes 1121280 | tf_op jit(solution)/shard_map/gkcm,gmcb->gkbm/dot_general | solution.py:50
  107.3 2.1 reshape.336
  109.5 7.5 %fusion.123 = f32[32,256,128]{2,1,0:T(8,128)S(1)} fusion(f32[32,256,16]{1,2,0:T(8,128)S(1)} %reshape.336, f32[32,16]{1,0:T(8,128)S(1)} %copy.40, f32[32,16]{1,0:T(8,128)S(1)} %copy.44), kind=kOutput, calls=%fused_computation.130 | convolution fusion | flops 201457664 | bytes 4722688 | tf_op jit(solution)/shard_map/dot_general | solution.py:59
  117.0 9.5 %add_convert_fusion = bf16[32,8,32,128]{3,2,1,0:T(8,128)(2,1)S(1)} fusion(f32[32,8,32,128]{3,2,1,0:T(8,128)S(1)} %bitcast.142, bf16[32,8,32,128]{3,2,1,0:T(8,128)(2,1)S(1)} %copy-done.4, f32[32]{0:T(128)S(1)} %get-tuple-element.29, f32[32]{0:T(128)S(1)} %get-tuple-element.13, f32[32]{0:T(128)S(1)} %get-tuple-element.30, f32[32]{0:T(128)S(1)} %get-tuple-element.14, ...), kind=kOutput, calls=%fused_computation.22 | convolution fusion | flops 1637875712 | bytes 8474624 | tf_op jit(solution)/shard_map/dot_general | solution.py:43
  126.5 6.8 %copy.50 = bf16[32,8,32,128]{0,1,3,2:T(8,128)(2,1)} copy(bf16[32,8,32,128]{3,2,1,0:T(8,128)(2,1)S(1)} %add_convert_fusion) | data formatting | bytes 4194304 | tf_op jit(solution)/shard_map/convert_element_type | solution.py:16
  133.3 10.1 %reshape.351 = bf16[8,2,65536]{2,1,0:T(2,128)(2,1)S(1)} reshape(bf16[4096,8,32]{2,1,0:T(8,128)(2,1)} %bitcast.140) | data formatting | bytes 4194304
  143.5 29.8 %all_to_all.24 = bf16[8,2,65536]{2,1,0:T(2,128)(2,1)} all-to-all(bf16[8,2,65536]{2,1,0:T(2,128)(2,1)S(1)} %reshape.351), channel_id=1, replica_groups=mesh['ctx'=8,'chan'=4] {'ctx'}, dimensions={0} | all-to-all | bytes 4194304 | tf_op jit(solution)/shard_map/all_to_all | solution.py:120
  173.2 8.7 %reshape.352 = bf16[4096,8,32]{2,1,0:T(8,128)(2,1)} reshape(bf16[8,2,65536]{2,1,0:T(2,128)(2,1)} %all_to_all.24) | data formatting | bytes 4194304
  181.9 10.2 %convert_bitcast_fusion = f32[8,32,8,512]{1,2,3,0:T(8,128)} fusion(bf16[32,8,8,512]{0,1,3,2:T(8,128)(2,1)} %bitcast.139), kind=kLoop, calls=%fused_computation | loop fusion | flops 1048576 | bytes 6291456 | tf_op jit(solution)/shard_map/convert_element_type | solution.py:122
  192.1 12.0 %copy.47 = f32[8,32,8,512]{3,2,1,0:T(8,128)} copy(f32[8,32,8,512]{1,2,3,0:T(8,128)} %convert_bitcast_fusion) | data formatting | bytes 8388608 | tf_op jit(solution)/shard_map/convert_element_type | solution.py:122
  204.1 6.4 %fusion.8 = bf16[2048,512]{1,0:T(8,128)(2,1)S(1)} fusion(f32[3,2048,512]{2,1,0:T(8,128)} %copy-done.2, f32[8,32,8,512]{3,2,1,0:T(8,128)} %copy.47, f32[2048]{0:T(1024)S(1)} %copy-done.6, pred[512]{0:T(512)(128)(4,1)S(1)} %iota_compare_fusion), kind=kLoop, calls=%fused_computation.16 | loop fusion | flops 7340032 | bytes 18883072 | tf_op jit(solution)/shard_map/convert_element_type | solution.py:126
  210.5 14.0 %fusion.5 = bf16[4096,512]{0,1:T(8,128)(2,1)} fusion(bf16[2048,512]{1,0:T(8,128)(2,1)S(1)} %fusion.8, bf16[2048,4096]{1,0:T(8,128)(2,1)} %param.15), kind=kOutput, calls=%fused_computation.11 | convolution fusion | flops 8592031744 | bytes 23068672 | tf_op jit(solution)/shard_map/dot_general | solution.py:128
  224.5 76.3 %reduce-scatter.2.cloned.1.call-done = bf16[1024,512]{0,1:T(8,128)(2,1)} async-done(((bf16[4096,512]{0,1:T(8,128)(2,1)}), bf16[1024,512]{0,1:T(8,128)(2,1)}) %reduce-scatter.2.cloned.1.call-update) | async-done | bytes 1048592 | tf_op jit(solution)/shard_map/reduce_scatter | solution.py:127
  300.8 2.3 copy.48
  (48 shorter events, 1.7 us)
Async XLA Ops:
  6.5 42.8 %copy-start = (f32[16,256]{1,0:T(8,128)S(1)}, f32[16,256]{1,0:T(8,128)}, u32[]{:S(2)}) copy-start(f32[16,256]{1,0:T(8,128)} %param.13) | copy-start | bytes 49156
  7.2 6.4 %copy-start.8 = (u32[32]{0:T(128)S(1)}, u32[32]{0:T(128)}, u32[]{:S(2)}) copy-start(u32[32]{0:T(128)} %constant.36) | copy-start | bytes 388
  7.2 17.6 %copy-start.5 = (f32[3,3,2048]{2,1,0:T(4,128)S(1)}, f32[3,3,2048]{2,1,0:T(4,128)}, u32[]{:S(2)}) copy-start(f32[3,3,2048]{2,1,0:T(4,128)} %param.9) | copy-start | bytes 221188
  10.6 14.5 %collective-permute-start = (bf16[3,2048,2]{1,0,2:T(4,128)(2,1)S(1)}, bf16[3,2048,2]{1,0,2:T(4,128)(2,1)S(1)}, u32[]{:S(2)}, u32[]{:S(2)}) collective-permute-start(bf16[3,2048,2]{1,0,2:T(4,128)(2,1)S(1)} %copy.54), channel_id=1, source_target_pairs={{0,4},{4,8},{8,12},{12,16},{16,20},{20,24},{24,28},{1,5},{5,9},{9,... | collective-permute-start | bytes 73736 | tf_op jit(solution)/shard_map/ppermute | solution.py:12
  38.5 4.5 %copy-start.2 = (f32[3,2048,512]{2,1,0:T(8,128)}, f32[3,2048,512]{2,1,0:T(8,128)S(1)}, u32[]{:S(2)}) copy-start(f32[3,2048,512]{2,1,0:T(8,128)S(1)} %multiply_add_fusion) | copy-start | bytes 37748740
  45.5 4.1 %copy-start.7 = (f32[16,256]{1,0:T(8,128)S(1)}, f32[16,256]{1,0:T(8,128)}, u32[]{:S(2)}) copy-start(f32[16,256]{1,0:T(8,128)} %param.12) | copy-start | bytes 49156
  45.5 30.3 %all-to-all-start = ((bf16[256,8,512]{2,1,0:T(8,128)(2,1)}), bf16[256,8,512]{2,1,0:T(8,128)(2,1)S(1)}, u32[]{:S(2)}, u32[]{:S(2)}) async-start(bf16[256,8,512]{2,1,0:T(8,128)(2,1)} %fusion.11), calls=%async_computation | async-start | bytes 4194304 | tf_op jit(solution)/shard_map/all_to_all | solution.py:106
  49.3 251.5 %reduce-scatter.2.cloned.1.call-start = ((), (), s32[]{:S(2)}) async-start(), calls=%async_computation.3 | async-start | bytes 5242880 | tf_op jit(solution)/shard_map/reduce_scatter | solution.py:127
  75.9 1.3 copy-start.3
  109.5 7.5 %copy-start.4 = (bf16[32,8,32,128]{3,2,1,0:T(8,128)(2,1)S(1)}, bf16[32,8,32,128]{3,2,1,0:T(8,128)(2,1)}, u32[]{:S(2)}) copy-start(bf16[32,8,32,128]{3,2,1,0:T(8,128)(2,1)} %reshape.334) | copy-start | bytes 6291460
  192.1 12.0 %copy-start.6 = (f32[2048]{0:T(1024)S(1)}, f32[2048]{0:T(1024)}, u32[]{:S(2)}) copy-start(f32[2048]{0:T(1024)} %param.14) | copy-start | bytes 24580
  224.5 78.6 %copy-start.1 = (f32[16,256]{1,0:T(8,128)S(1)}, f32[16,256]{1,0:T(8,128)}, u32[]{:S(2)}) copy-start(f32[16,256]{1,0:T(8,128)} %param.13) | copy-start | bytes 49156
Sparse Core Ops, SparseCore 0:
  224.6 76.1 reduce-scatter.1
where the time goes:
time: 311 us; the launch traced here: 310 us
  waiting for transfers between devices  102 us (33%)
  local copies, waits for them, and re-layouts  63.9 us (21%)
  matrix products  52 us (17%)
  blocking collectives  38.8 us (12%)
  other arithmetic  32.2 us (10%)
  between operations  15 us (5%)
  starting transfers between devices  6.13 us (2%)
    reduce_scatter x1, waiting for transfers between devices, shards(): lax.psum_scatter(lax.dot_general(out_weight, mixed_rows, (((0,), (0,)), (...  76.3 us
    all_to_all x1, blocking collectives, shards(): lax.all_to_all(shortened(result), 'ctx', split_axis=2, concat_axis=0, til...  29.8 us
    unnamed x28, local copies, waits for them, and re-layouts  27.7 us
    all_to_all x1, waiting for transfers between devices, shards(): lax.all_to_all(product.reshape(groups, per_group, slot_count).astype(jnp....  25.6 us
    dot_general x1, matrix products, block_pass(): entering = jnp.einsum('gkcm,gmcb->gkbm', summary, mixing, precision=highest)  17.6 us
    dot_general x1, matrix products, shards(): lax.dot_general(out_weight, mixed_rows, (((0,), (0,)), ((), ())), preferr...  14 us
    add x1, other arithmetic, shards(): short_conv + short_filter[:, tap_index, :, None] * window_rows.astype(jnp...  12.5 us
    convert_element_type x1, local copies, waits for them, and re-layouts, shards(): long_conv = lax.all_to_all(shortened(result), 'ctx', split_axis=2, concat...  12 us
  transfers between devices with their start and end apart: 3, of which 2 were waited for; matrix products, arithmetic and copies ran while one was open for 1% of the time, Pallas kernels for 0%

commit v1 on v0

--- a/solution.py
+++ b/solution.py
@@ -4,6 +4,29 @@
 from jax.sharding import PartitionSpec as P
 
 highest = lax.Precision.HIGHEST
+
+
+def split_up(shard, dim, size):
+    lengths = shard.shape
+    blocks = shard.reshape(*lengths[:dim], size, lengths[dim] // size, *lengths[dim + 1 :])
+    return jnp.moveaxis(blocks, dim, 0)
+
+
+def joined_along(parts, dim):
+    parts = jnp.moveaxis(parts, 0, dim)
+    lengths = parts.shape
+    return parts.reshape(*lengths[:dim], lengths[dim] * lengths[dim + 1], *lengths[dim + 2 :])
+
+
+def exchange_directly(shard, axis, split_dim, concat_dim):
+    size, index = (lax.axis_size(axis), lax.axis_index(axis))
+    blocks = split_up(shard, split_dim, size)
+    finished = [blocks[index]]
+    for step in range(1, size):
+        sent = blocks[(index + step) % size]
+        finished.append(lax.ppermute(sent, axis, [(i, (i + step) % size) for i in range(size)]))
+    blocks = jnp.stack(finished)[(index - jnp.arange(size)) % size]
+    return joined_along(blocks, concat_dim)
 
 
 def passed_along(array, axis, by):
@@ -103,12 +126,8 @@
     within = jnp.tile(jnp.arange(per_shard) * block_width, ctx_count)
     firsts_all = jnp.repeat(all_offsets, per_shard).astype(jnp.float32) + within.astype(jnp.float32)
     counts_all = jnp.clip(jnp.repeat(all_lengths, per_shard) - within, 0, block_width)
-    received = lax.all_to_all(
-        product.reshape(groups, per_group, slot_count).astype(jnp.bfloat16),
-        "ctx",
-        split_axis=0,
-        concat_axis=2,
-        tiled=True,
+    received = exchange_directly(
+        product.reshape(groups, per_group, slot_count).astype(jnp.bfloat16), "ctx", 0, 2
     ).astype(jnp.float32)
     item_count = received.shape[1]
     blocks = received.reshape(shared, item_count, ctx_count * per_shard, block_width)

time: 311 us -> 315 us (1.013)
  waiting for transfers between devices: 102 us -> 92.4 us
  blocking collectives: 38.8 us -> 43.6 us
  local copies, waits for them, and re-layouts: 63.9 us -> 67.5 us
    all_to_all x1 -> x0, waiting for transfers between devices: 25.6 us -> none  [shards(): lax.all_to_all(product.reshape(groups, per_group, slot_count).astype(jnp....]
    ppermute x0 -> x7, waiting for transfers between devices: none -> 16.2 us  [exchange_directly(): lax.ppermute(sent, axis, [(i, (i + step) % size) for i in range(size)])]
    ppermute x0 -> x7, starting transfers between devices: none -> 6.04 us  [exchange_directly(): lax.ppermute(sent, axis, [(i, (i + step) % size) for i in range(size)])]
    all_to_all x1, blocking collectives: 29.8 us -> 34.6 us  [shards(): lax.all_to_all(shortened(result), 'ctx', split_axis=2, concat_axis=0, til...]
    all_to_all x1 -> x0, starting transfers between devices: 3.73 us -> none  [shards(): lax.all_to_all(product.reshape(groups, per_group, slot_count).astype(jnp....]
    all_to_all x1 -> x0, local copies, waits for them, and re-layouts: 3.31 us -> none  [shards(): lax.all_to_all(product.reshape(groups, per_group, slot_count).astype(jnp....]
    transpose x0 -> x1, local copies, waits for them, and re-layouts: none -> 3.31 us  [joined_along(): parts = jnp.moveaxis(parts, 0, dim)]
    unnamed x28 -> x106, local copies, waits for them, and re-layouts: 27.7 us -> 27.5 us
  transfers between devices with their start and end apart: 3 -> 9, of which waited for: 2 -> 5; matrix products, arithmetic and copies ran while one was open for 1% -> 3% of each run, Pallas kernels for 0% -> 0%
where the time goes in v1:
time: 315 us; the launch traced here: 314 us
  waiting for transfers between devices  92.4 us (29%)
  local copies, waits for them, and re-layouts  67.5 us (21%)
  matrix products  52 us (17%)
  blocking collectives  43.6 us (14%)
  other arithmetic  34.5 us (11%)
  between operations  15.6 us (5%)
  starting transfers between devices  8.4 us (3%)
    reduce_scatter x1, waiting for transfers between devices, shards(): lax.psum_scatter(lax.dot_general(out_weight, mixed_rows, (((0,), (0,)), (...  76.3 us
    all_to_all x1, blocking collectives, shards(): lax.all_to_all(shortened(result), 'ctx', split_axis=2, concat_axis=0, til...  34.6 us
    unnamed x106, local copies, waits for them, and re-layouts  27.5 us
    dot_general x1, matrix products, block_pass(): entering = jnp.einsum('gkcm,gmcb->gkbm', summary, mixing, precision=highest)  17.6 us
    ppermute x7, waiting for transfers between devices, exchange_directly(): lax.ppermute(sent, axis, [(i, (i + step) % size) for i in range(size)])  16.2 us
    dot_general x1, matrix products, shards(): lax.dot_general(out_weight, mixed_rows, (((0,), (0,)), ((), ())), preferr...  13.9 us
    add x1, other arithmetic, shards(): short_conv + short_filter[:, tap_index, :, None] * window_rows.astype(jnp...  12.5 us
    convert_element_type x1, local copies, waits for them, and re-layouts, shards(): long_conv = lax.all_to_all(shortened(result), 'ctx', split_axis=2, concat...  12 us
  transfers between devices with their start and end apart: 9, of which 5 were waited for; matrix products, arithmetic and copies ran while one was open for 3% of the time, Pallas kernels for 0%

profile of v1, /device:TPU:0, one launch (start us, length us, event | category | flops | bytes accessed | tf_op | source)
XLA Modules:
  0.0 314.1 jit_solution(4872482775466631838)
XLA Ops:
  7.2 2.5 constant_dynamic-slice_fusion
  10.6 2.4 collective-permute-start
  16.6 9.1 %all-reduce.2 = (s32[8]{0:T(128)S(1)}, s32[8]{0:T(128)S(1)}) all-reduce(s32[8]{0:T(128)S(1)} %dynamic-update-slice, s32[8]{0:T(128)S(1)} %dynamic-update-slice.1), channel_id=1, replica_groups=mesh['ctx'=8,'chan'=4] {'ctx'}, use_global_device_ids=true, to_apply=%add | all-reduce | flops 16 | bytes 128
  29.4 12.5 %multiply_add_fusion = f32[3,2048,512]{2,1,0:T(8,128)S(1)} fusion(bf16[3,2048,512]{2,1,0:T(8,128)(2,1)} %param.8, bf16[3,2048,2]{2,1,0:T(8,128)(2,1)S(1)} %copy.40, f32[3,2048]{1,0:T(4,128)S(1)} %get-tuple-element.54, f32[3,2048]{1,0:T(4,128)S(1)} %get-tuple-element.55, f32[3,2048]{1,0:T(4,128)S(1)} %bitcast.169), kind=kLoop, calls=%fused_computation.2 | loop fusion | flops 44040192 | bytes 18972672 | tf_op jit(solution)/shard_map/add | solution.py:111
  42.0 1.1 slice_multiply_fusion
  43.0 3.5 %copy-done.2 = f32[3,2048,512]{2,1,0:T(8,128)} copy-done((f32[3,2048,512]{2,1,0:T(8,128)}, f32[3,2048,512]{2,1,0:T(8,128)S(1)}, u32[]{:S(2)}) %copy-start.2) | copy-done | bytes 12582936
  47.1 1.0 dynamic-slice_bitcast_fusion
  48.7 1.7 collective-permute-start.2
  51.1 2.4 collective-permute-start.7
  53.8 2.8 collective-permute-done.1
  57.6 1.7 collective-permute-done.2
  59.3 1.6 collective-permute-start.4
  61.9 11.1 %collective-permute-done.3 = bf16[32,8,512]{2,1,0:T(8,128)(2,1)S(1)} collective-permute-done((bf16[32,8,512]{2,1,0:T(8,128)(2,1)S(1)}, bf16[32,8,512]{2,1,0:T(8,128)(2,1)S(1)}, u32[]{:S(2)}, u32[]{:S(2)}) %collective-permute-start.3) | collective-permute-done | bytes 262176 | tf_op jit(solution)/shard_map/ppermute | solution.py:27
  73.7 2.1 gather_fusion
  75.8 3.3 %copy.41 = bf16[32,8,8,512]{3,2,1,0:T(8,128)(2,1)S(1)} copy(bf16[32,8,8,512]{3,1,0,2:T(8,128)(2,1)} %bitcast.167) | data formatting | bytes 4194304 | tf_op jit(solution)/shard_map/transpose | solution.py:16
  79.1 2.8 reshape_reshape.3
  81.9 2.6 reshape.387
  84.5 3.4 %fusion.127 = f32[32,256,16]{1,2,0:T(8,128)S(1)} fusion(bf16[32,256,128]{2,1,0:T(8,128)(2,1)} %reshape_reshape.3, f32[128]{0:T(128)S(1)} %copy-done.43, f32[32,16]{1,0:T(8,128)S(1)} %copy.42), kind=kOutput, calls=%fused_computation.143 | convolution fusion | flops 201392128 | bytes 2624000 | tf_op jit(solution)/shard_map/dot_general | solution.py:50
  88.4 17.6 %fusion.81 = f32[32,8,32,16]{2,1,3,0:T(8,128)} fusion(f32[32,8,32,16]{2,1,3,0:T(8,128)S(1)} %reshape.388, f32[32,32]{1,0:T(8,128)S(1)} %subtract_maximum_fusion, f32[32,16]{1,0:T(8,128)S(1)} %copy.42, pred[32,32]{1,0:T(8,128)(4,1)S(1)} %copy-done.8, f32[32,32,16]{1,2,0:T(8,128)S(1)} %copy-done.4), kind=kOutput, calls=%fused_computation.93 | convolution fusion | flops 51511296 | bytes 1121280 | tf_op jit(solution)/shard_map/gkcm,gmcb->gkbm/dot_general | solution.py:73
  106.0 2.1 reshape.389
  108.5 7.5 %fusion.122 = f32[32,256,128]{2,1,0:T(8,128)S(1)} fusion(f32[32,256,16]{1,2,0:T(8,128)S(1)} %reshape.389, f32[32,16]{1,0:T(8,128)S(1)} %copy.42, f32[32,16]{1,0:T(8,128)S(1)} %copy.46), kind=kOutput, calls=%fused_computation.137 | convolution fusion | flops 201457664 | bytes 4722688 | tf_op jit(solution)/shard_map/dot_general | solution.py:82
  116.4 9.5 %add_convert_fusion = bf16[32,8,32,128]{3,2,1,0:T(8,128)(2,1)S(1)} fusion(f32[32,8,32,128]{3,2,1,0:T(8,128)S(1)} %bitcast.168, bf16[32,8,32,128]{3,2,1,0:T(8,128)(2,1)S(1)} %copy-done.3, f32[32]{0:T(128)S(1)} %copy-done.12, f32[32]{0:T(128)S(1)} %copy-done.28, f32[32]{0:T(128)S(1)} %copy-done.13, f32[32]{0:T(128)S(1)} %copy-done.29, f32[32]{0:T(128)S(1)} %copy-done.14, ...), kind=kOutput, calls=%fused_computation.21 | convolution fusion | flops 1637875712 | bytes 8474624 | tf_op jit(solution)/shard_map/dot_general | solution.py:66
  125.9 6.8 %copy.52 = bf16[32,8,32,128]{0,1,3,2:T(8,128)(2,1)} copy(bf16[32,8,32,128]{3,2,1,0:T(8,128)(2,1)S(1)} %add_convert_fusion) | data formatting | bytes 4194304 | tf_op jit(solution)/shard_map/convert_element_type | solution.py:39
  132.7 10.1 %reshape.412 = bf16[8,2,65536]{2,1,0:T(2,128)(2,1)S(1)} reshape(bf16[4096,8,32]{2,1,0:T(8,128)(2,1)} %bitcast.165) | data formatting | bytes 4194304
  142.9 34.6 %all_to_all.4 = bf16[8,2,65536]{2,1,0:T(2,128)(2,1)} all-to-all(bf16[8,2,65536]{2,1,0:T(2,128)(2,1)S(1)} %reshape.412), channel_id=1, replica_groups=mesh['ctx'=8,'chan'=4] {'ctx'}, dimensions={0} | all-to-all | bytes 4194304 | tf_op jit(solution)/shard_map/all_to_all | solution.py:139
  177.5 8.7 %reshape.413 = bf16[4096,8,32]{2,1,0:T(8,128)(2,1)} reshape(bf16[8,2,65536]{2,1,0:T(2,128)(2,1)} %all_to_all.4) | data formatting | bytes 4194304
  186.1 10.3 %convert_bitcast_fusion = f32[8,32,8,512]{1,2,3,0:T(8,128)} fusion(bf16[32,8,8,512]{0,1,3,2:T(8,128)(2,1)} %bitcast.164), kind=kLoop, calls=%fused_computation.1 | loop fusion | flops 1048576 | bytes 6291456 | tf_op jit(solution)/shard_map/convert_element_type | solution.py:141
  196.4 12.0 %copy.49 = f32[8,32,8,512]{3,2,1,0:T(8,128)} copy(f32[8,32,8,512]{1,2,3,0:T(8,128)} %convert_bitcast_fusion) | data formatting | bytes 8388608 | tf_op jit(solution)/shard_map/convert_element_type | solution.py:141
  208.4 6.4 %fusion.8 = bf16[2048,512]{1,0:T(8,128)(2,1)S(1)} fusion(f32[3,2048,512]{2,1,0:T(8,128)} %copy-done.2, f32[8,32,8,512]{3,2,1,0:T(8,128)} %copy.49, f32[2048]{0:T(1024)S(1)} %copy-done.6, pred[512]{0:T(512)(128)(4,1)S(1)} %copy-done.10), kind=kLoop, calls=%fused_computation.17 | loop fusion | flops 7340032 | bytes 18883072 | tf_op jit(solution)/shard_map/convert_element_type | solution.py:145
  214.8 13.9 %fusion.5 = bf16[4096,512]{0,1:T(8,128)(2,1)} fusion(bf16[2048,512]{1,0:T(8,128)(2,1)S(1)} %fusion.8, bf16[2048,4096]{1,0:T(8,128)(2,1)} %param.15), kind=kOutput, calls=%fused_computation.12 | convolution fusion | flops 8592031744 | bytes 23068672 | tf_op jit(solution)/shard_map/dot_general | solution.py:147
  228.7 76.3 %reduce-scatter.2.cloned.1.call-done = bf16[1024,512]{0,1:T(8,128)(2,1)} async-done(((bf16[4096,512]{0,1:T(8,128)(2,1)}), bf16[1024,512]{0,1:T(8,128)(2,1)}) %reduce-scatter.2.cloned.1.call-update) | async-done | bytes 1048592 | tf_op jit(solution)/shard_map/reduce_scatter | solution.py:146
  305.0 2.3 copy.50
  (144 shorter events, 13.0 us)
Async XLA Ops:
  6.5 20.2 %copy-start = (f32[16,256]{1,0:T(8,128)S(1)}, f32[16,256]{1,0:T(8,128)}, u32[]{:S(2)}) copy-start(f32[16,256]{1,0:T(8,128)} %param.13) | copy-start | bytes 49156
  6.5 298.5 %reduce-scatter.2.cloned.1.call-start = ((), (), s32[]{:S(2)}) async-start(), calls=%async_computation.2 | async-start | bytes 5242880 | tf_op jit(solution)/shard_map/reduce_scatter | solution.py:146
  7.2 20.3 %copy-start.5 = (f32[3,3,2048]{2,1,0:T(4,128)S(1)}, f32[3,3,2048]{2,1,0:T(4,128)}, u32[]{:S(2)}) copy-start(f32[3,3,2048]{2,1,0:T(4,128)} %param.9) | copy-start | bytes 221188
  10.6 17.9 %collective-permute-start = (bf16[3,2048,2]{1,0,2:T(4,128)(2,1)S(1)}, bf16[3,2048,2]{1,0,2:T(4,128)(2,1)S(1)}, u32[]{:S(2)}, u32[]{:S(2)}) collective-permute-start(bf16[3,2048,2]{1,0,2:T(4,128)(2,1)S(1)} %copy.56), channel_id=1, source_target_pairs={{0,4},{4,8},{8,12},{12,16},{16,20},{20,24},{24,28},{1,5},{5,9},{9,... | collective-permute-start | bytes 73736 | tf_op jit(solution)/shard_map/ppermute | solution.py:35
  28.4 18.1 %copy-start.9 = (pred[512]{0:T(512)(128)(4,1)}, pred[512]{0:T(512)(128)(4,1)S(1)}, u32[]{:S(2)}) copy-start(pred[512]{0:T(512)(128)(4,1)S(1)} %iota_compare_fusion) | copy-start | bytes 1540
  48.1 8.5 %collective-permute-start.1 = (bf16[32,8,512]{2,1,0:T(8,128)(2,1)}, bf16[32,8,512]{2,1,0:T(8,128)(2,1)}, u32[]{:S(2)}, u32[]{:S(2)}) collective-permute-start(bf16[32,8,512]{2,1,0:T(8,128)(2,1)} %get-tuple-element.15), channel_id=1, source_target_pairs={{0,4},{4,8},{8,12},{12,16},{16,20},{20,24},{24,28},{28,0},{1,5},{5... | collective-permute-start | bytes 786440 | tf_op jit(solution)/shard_map/ppermute | solution.py:27
  48.7 10.6 %collective-permute-start.2 = (bf16[32,8,512]{2,1,0:T(8,128)(2,1)}, bf16[32,8,512]{2,1,0:T(8,128)(2,1)}, u32[]{:S(2)}, u32[]{:S(2)}) collective-permute-start(bf16[32,8,512]{2,1,0:T(8,128)(2,1)} %get-tuple-element.14), channel_id=1, source_target_pairs={{0,8},{4,12},{8,16},{12,20},{16,24},{20,28},{24,0},{28,4},{1,9},{5... | collective-permute-start | bytes 786440 | tf_op jit(solution)/shard_map/ppermute | solution.py:27
  51.1 22.6 %collective-permute-start.7 = (bf16[32,8,512]{2,1,0:T(8,128)(2,1)S(1)}, bf16[32,8,512]{2,1,0:T(8,128)(2,1)S(1)}, u32[]{:S(2)}, u32[]{:S(2)}) collective-permute-start(bf16[32,8,512]{2,1,0:T(8,128)(2,1)S(1)} %get-tuple-element.9), channel_id=1, source_target_pairs={{0,28},{4,0},{8,4},{12,8},{16,12},{20,16},{24,20},{28,24},{1,29},{... | collective-permute-start | bytes 786440 | tf_op jit(solution)/shard_map/ppermute | solution.py:27
  53.4 20.2 %collective-permute-start.6 = (bf16[32,8,512]{2,1,0:T(8,128)(2,1)S(1)}, bf16[32,8,512]{2,1,0:T(8,128)(2,1)S(1)}, u32[]{:S(2)}, u32[]{:S(2)}) collective-permute-start(bf16[32,8,512]{2,1,0:T(8,128)(2,1)S(1)} %get-tuple-element.10), channel_id=1, source_target_pairs={{0,24},{4,28},{8,0},{12,4},{16,8},{20,12},{24,16},{28,20},{1,25},{... | collective-permute-start | bytes 786440 | tf_op jit(solution)/shard_map/ppermute | solution.py:27
  53.8 19.7 %collective-permute-start.5 = (bf16[32,8,512]{2,1,0:T(8,128)(2,1)S(1)}, bf16[32,8,512]{2,1,0:T(8,128)(2,1)S(1)}, u32[]{:S(2)}, u32[]{:S(2)}) collective-permute-start(bf16[32,8,512]{2,1,0:T(8,128)(2,1)S(1)} %get-tuple-element.11), channel_id=1, source_target_pairs={{0,20},{4,24},{8,28},{12,0},{16,4},{20,8},{24,12},{28,16},{1,21},{... | collective-permute-start | bytes 786440 | tf_op jit(solution)/shard_map/ppermute | solution.py:27
  56.7 16.3 %collective-permute-start.3 = (bf16[32,8,512]{2,1,0:T(8,128)(2,1)S(1)}, bf16[32,8,512]{2,1,0:T(8,128)(2,1)S(1)}, u32[]{:S(2)}, u32[]{:S(2)}) collective-permute-start(bf16[32,8,512]{2,1,0:T(8,128)(2,1)S(1)} %get-tuple-element.13), channel_id=1, source_target_pairs={{0,12},{4,16},{8,20},{12,24},{16,28},{20,0},{24,4},{28,8},{1,13},{... | collective-permute-start | bytes 786440 | tf_op jit(solution)/shard_map/ppermute | solution.py:27
  59.3 13.7 %collective-permute-start.4 = (bf16[32,8,512]{2,1,0:T(8,128)(2,1)S(1)}, bf16[32,8,512]{2,1,0:T(8,128)(2,1)S(1)}, u32[]{:S(2)}, u32[]{:S(2)}) collective-permute-start(bf16[32,8,512]{2,1,0:T(8,128)(2,1)S(1)} %get-tuple-element.12), channel_id=1, source_target_pairs={{0,16},{4,20},{8,24},{12,28},{16,0},{20,4},{24,8},{28,12},{1,17},{... | collective-permute-start | bytes 786440 | tf_op jit(solution)/shard_map/ppermute | solution.py:27
  108.2 7.9 %copy-start.3 = (bf16[32,8,32,128]{3,2,1,0:T(8,128)(2,1)S(1)}, bf16[32,8,32,128]{3,2,1,0:T(8,128)(2,1)}, u32[]{:S(2)}) copy-start(bf16[32,8,32,128]{3,2,1,0:T(8,128)(2,1)} %reshape.387) | copy-start | bytes 6291460
  108.2 7.9 %copy-start.11 = (f32[32]{0:T(128)S(1)}, f32[32]{0:T(128)}, u32[]{:S(2)}) copy-start(f32[32]{0:T(128)} %get-tuple-element.36) | copy-start | bytes 388
  108.2 7.9 %copy-start.12 = (f32[32]{0:T(128)S(1)}, f32[32]{0:T(128)}, u32[]{:S(2)}) copy-start(f32[32]{0:T(128)} %get-tuple-element.37) | copy-start | bytes 388
  108.2 7.9 %copy-start.13 = (f32[32]{0:T(128)S(1)}, f32[32]{0:T(128)}, u32[]{:S(2)}) copy-start(f32[32]{0:T(128)} %get-tuple-element.38) | copy-start | bytes 388
  108.2 7.9 %copy-start.14 = (f32[32]{0:T(128)S(1)}, f32[32]{0:T(128)}, u32[]{:S(2)}) copy-start(f32[32]{0:T(128)} %get-tuple-element.39) | copy-start | bytes 388
  108.2 7.9 %copy-start.15 = (f32[32]{0:T(128)S(1)}, f32[32]{0:T(128)}, u32[]{:S(2)}) copy-start(f32[32]{0:T(128)} %get-tuple-element.40) | copy-start | bytes 388
  108.2 7.9 %copy-start.16 = (f32[32]{0:T(128)S(1)}, f32[32]{0:T(128)}, u32[]{:S(2)}) copy-start(f32[32]{0:T(128)} %get-tuple-element.41) | copy-start | bytes 388
  108.3 7.9 %copy-start.17 = (f32[32]{0:T(128)S(1)}, f32[32]{0:T(128)}, u32[]{:S(2)}) copy-start(f32[32]{0:T(128)} %get-tuple-element.42) | copy-start | bytes 388
  108.3 7.9 %copy-start.18 = (f32[32]{0:T(128)S(1)}, f32[32]{0:T(128)}, u32[]{:S(2)}) copy-start(f32[32]{0:T(128)} %get-tuple-element.43) | copy-start | bytes 388
  108.3 7.9 %copy-start.19 = (f32[32]{0:T(128)S(1)}, f32[32]{0:T(128)}, u32[]{:S(2)}) copy-start(f32[32]{0:T(128)} %get-tuple-element.44) | copy-start | bytes 388
  108.3 7.9 %copy-start.20 = (f32[32]{0:T(128)S(1)}, f32[32]{0:T(128)}, u32[]{:S(2)}) copy-start(f32[32]{0:T(128)} %get-tuple-element.45) | copy-start | bytes 388
  108.3 7.9 %copy-start.21 = (f32[32]{0:T(128)S(1)}, f32[32]{0:T(128)}, u32[]{:S(2)}) copy-start(f32[32]{0:T(128)} %get-tuple-element.46) | copy-start | bytes 388
  108.3 7.9 %copy-start.22 = (f32[32]{0:T(128)S(1)}, f32[32]{0:T(128)}, u32[]{:S(2)}) copy-start(f32[32]{0:T(128)} %get-tuple-element.47) | copy-start | bytes 388
  108.3 7.9 %copy-start.23 = (f32[32]{0:T(128)S(1)}, f32[32]{0:T(128)}, u32[]{:S(2)}) copy-start(f32[32]{0:T(128)} %get-tuple-element.48) | copy-start | bytes 388
  108.3 7.9 %copy-start.24 = (f32[32]{0:T(128)S(1)}, f32[32]{0:T(128)}, u32[]{:S(2)}) copy-start(f32[32]{0:T(128)} %get-tuple-element.49) | copy-start | bytes 388
  108.3 7.9 %copy-start.25 = (f32[32]{0:T(128)S(1)}, f32[32]{0:T(128)}, u32[]{:S(2)}) copy-start(f32[32]{0:T(128)} %get-tuple-element.50) | copy-start | bytes 388
  108.3 7.9 %copy-start.26 = (f32[32]{0:T(128)S(1)}, f32[32]{0:T(128)}, u32[]{:S(2)}) copy-start(f32[32]{0:T(128)} %get-tuple-element.51) | copy-start | bytes 388
  196.4 12.0 %copy-start.6 = (f32[2048]{0:T(1024)S(1)}, f32[2048]{0:T(1024)}, u32[]{:S(2)}) copy-start(f32[2048]{0:T(1024)} %param.14) | copy-start | bytes 24580
  196.4 12.0 %copy-start.10 = (pred[512]{0:T(512)(128)(4,1)S(1)}, pred[512]{0:T(512)(128)(4,1)}, u32[]{:S(2)}) copy-start(pred[512]{0:T(512)(128)(4,1)} %copy-done.9) | copy-start | bytes 1540
  228.7 78.6 %copy-start.1 = (f32[16,256]{1,0:T(8,128)S(1)}, f32[16,256]{1,0:T(8,128)}, u32[]{:S(2)}) copy-start(f32[16,256]{1,0:T(8,128)} %param.13) | copy-start | bytes 49156
  (22 other events, 154.6 us)
Sparse Core Ops, SparseCore 0:
  228.8 76.1 reduce-scatter.1
